TPU v7x, 512 devices: a whole 4x8x8 slice. The times are simulated.
512 devices in a mesh: head: 8 (over x, core), blk: 64 (over y, z).
Axes of the slice: x: 4, y: 8, z: 8, core: 2. Of those that a mesh axis runs over, the one named last changes fastest.
Arguments:
- suffix_hidden: bfloat16 [1536, 2048], P('blk'), may hold values from -400 to 400
- prefix_hidden: bfloat16 [16384, 2048], P('blk'), may hold values from -400 to 400
- kv_cache: bfloat16 [2, 16384, 8, 256], P(None, 'blk', 'head'), may hold values from -300 to 300
- norm_gain: float32 [2048], replicated, may hold values from 0.1 to 1.9
- norm_bias: float32 [2048], replicated, may hold values from -3 to 3
- qkv_weight: bfloat16 [2048, 8, 768], P('blk', 'head'), may hold values from -0.125 to 0.125
- qkv_bias: float32 [8, 768], P('head'), may hold values from -3 to 3
- out_weight: bfloat16 [8, 256, 2048], P('head', 'blk'), may hold values from -0.125 to 0.125
- out_bias: float32 [2048], replicated, may hold values from -3 to 3
- suffix_lengths: int32 [4], replicated, may hold values from 1 to 768, 1536 in all
- prefix_blocks: int32 [4], replicated, may hold values from 1 to 32, 64 in all
- block_owner: int32 [64], replicated, may hold values from 0 to 63, each once
- recompute_flag: int32 [16384], P('blk'), may hold values from 0 to 1, as said below
Outputs:
- attn_out: bfloat16 [1536, 2048], P('blk', 'head')
Inputs may be any that keep to these rules, and one draw needn't show every extreme that they name: `recompute_flag`: each storage block of 256 cache rows holds exactly 25 ones.
All inputs are finite; a program needn't handle non-finite values.
Results may differ from a plain program's by a relative error of at most 0.015.
Values may be sent and summed in bfloat16 or wider, within the bound.
A program may use at most 64 MiB of HBM per device.

v0:
```python
import math
import jax
import jax.numpy as jnp
from jax import lax
from jax.sharding import PartitionSpec as P

FLAG_DEV = 25
EPSILON = 1e-05
MASKED = -1e30


def layer_norm(states, norm_scale, norm_shift):
    widened = states.astype(jnp.float32)
    average = jnp.mean(widened, axis=-1, keepdims=True)
    center = widened - average
    variance = jnp.mean(center * center, axis=-1, keepdims=True)
    return (center * lax.rsqrt(variance + EPSILON) * norm_scale + norm_shift).astype(jnp.bfloat16)


def body(
    suffix_hidden,
    prefix_hidden,
    kv_cache,
    norm_gain,
    norm_bias,
    qkv_weight,
    qkv_bias,
    out_weight,
    out_bias,
    suffix_lengths,
    prefix_blocks,
    block_owner,
    recompute_flag,
):
    blk_total = lax.axis_size("blk")
    own_index = lax.axis_index("blk")
    row_count = suffix_hidden.shape[0]
    cache_rows = prefix_hidden.shape[0]
    heads_dev = qkv_weight.shape[1]
    head_dim = qkv_weight.shape[2] // 3
    total_rows = row_count * blk_total
    own_first = own_index * row_count
    tenant_ends = jnp.cumsum(suffix_lengths)
    row_ids = jnp.arange(total_rows, dtype=jnp.int32)
    row_tenant = jnp.sum((row_ids[:, None] >= tenant_ends[None, :]).astype(jnp.int32), axis=1)
    block_ends = jnp.cumsum(prefix_blocks)
    block_slots = jnp.arange(blk_total, dtype=jnp.int32)
    global_block = jnp.sum(jnp.where(block_owner == own_index, block_slots, 0))
    block_tenant = jnp.sum((global_block >= block_ends).astype(jnp.int32))
    normed = layer_norm(suffix_hidden, norm_gain, norm_bias)
    flagged = jnp.argsort(1 - recompute_flag, stable=True)[:FLAG_DEV]
    prefix_normed = layer_norm(prefix_hidden[flagged], norm_gain, norm_bias)
    qkv_rows = qkv_weight.shape[0]
    out_rows = out_weight.shape[1]
    model_dim = out_weight.shape[2]
    packed_weights = jnp.concatenate([qkv_weight.reshape(1, -1), out_weight.reshape(1, -1)], axis=1)
    fetched_all = lax.all_gather(packed_weights, "blk", axis=0, tiled=True)
    qkv_size = qkv_rows * heads_dev * 3 * head_dim
    fetched = fetched_all[:, :qkv_size].reshape(blk_total * qkv_rows, heads_dev, 3 * head_dim)
    out_fetched = fetched_all[:, qkv_size:].reshape(blk_total, heads_dev, out_rows, model_dim)
    out_fetched = jnp.transpose(out_fetched, (1, 0, 2, 3)).reshape(
        heads_dev, blk_total * out_rows, model_dim
    )
    piece_rows = fetched.shape[0]
    flattened = fetched.reshape(piece_rows, heads_dev * 3 * head_dim)
    kv_part = fetched[:, :, head_dim:].reshape(piece_rows, heads_dev * 2 * head_dim)
    suffix_acc = jnp.dot(normed, flattened, preferred_element_type=jnp.float32)
    prefix_acc = jnp.dot(prefix_normed, kv_part, preferred_element_type=jnp.float32)
    suffix_acc, prefix_acc = (suffix_acc, prefix_acc)
    projected = (
        (suffix_acc + qkv_bias.reshape(-1))
        .astype(jnp.bfloat16)
        .reshape(row_count, heads_dev, 3 * head_dim)
    )
    recomputed = (
        (prefix_acc + qkv_bias[:, head_dim:].reshape(-1))
        .astype(jnp.bfloat16)
        .reshape(FLAG_DEV, heads_dev, 2 * head_dim)
    )
    own_queries = projected[:, :, :head_dim].reshape(row_count, heads_dev * head_dim)
    gathered = lax.all_gather(own_queries, "blk", axis=0, tiled=True)
    prefix_keys = kv_cache[0].at[flagged].set(recomputed[:, :, :head_dim])
    prefix_values = kv_cache[1].at[flagged].set(recomputed[:, :, head_dim:])
    keys_all = jnp.concatenate([prefix_keys, projected[:, :, head_dim : 2 * head_dim]], axis=0)
    values_all = jnp.concatenate([prefix_values, projected[:, :, 2 * head_dim :]], axis=0)
    own_tenant = lax.dynamic_slice_in_dim(row_tenant, own_first, row_count, 0)
    key_tenant = jnp.concatenate([jnp.full((cache_rows,), block_tenant, jnp.int32), own_tenant])
    key_position = jnp.concatenate(
        [jnp.full((cache_rows,), -1, jnp.int32), own_first + jnp.arange(row_count, dtype=jnp.int32)]
    )
    scale = head_dim ** (-0.5)
    qblock = math.gcd(total_rows, 512)
    block_total = total_rows // qblock

    def partial_block(offset):
        query_block = lax.dynamic_slice_in_dim(gathered, offset, qblock, 0).reshape(
            qblock, heads_dev, head_dim
        )
        query_tenant = lax.dynamic_slice_in_dim(row_tenant, offset, qblock, 0)
        query_position = offset + jnp.arange(qblock, dtype=jnp.int32)
        allowed = (query_tenant[:, None] == key_tenant[None, :]) & (
            key_position[None, :] <= query_position[:, None]
        )
        scores = (
            jnp.einsum("qhd,khd->hqk", query_block, keys_all, preferred_element_type=jnp.float32)
            * scale
        )
        gate = allowed[None, :, :]
        row_peak = jnp.max(jnp.where(gate, scores, MASKED), axis=2)
        weights = jnp.where(gate, jnp.exp(scores - row_peak[:, :, None]), 0.0)
        denominator = jnp.sum(weights, axis=2)
        numerator = jnp.einsum(
            "hqk,khd->qhd",
            weights.astype(jnp.bfloat16),
            values_all,
            preferred_element_type=jnp.float32,
        )
        return (numerator.reshape(qblock, heads_dev * head_dim), denominator.T, row_peak.T)

    def fill_block(step_index, buffers):
        numer_buf, denom_buf, peak_buf = buffers
        offset = step_index * qblock
        numerator, denominator, row_peak = partial_block(offset)
        numer_buf = lax.dynamic_update_slice_in_dim(numer_buf, numerator, offset, 0)
        denom_buf = lax.dynamic_update_slice_in_dim(denom_buf, denominator, offset, 0)
        peak_buf = lax.dynamic_update_slice_in_dim(peak_buf, row_peak, offset, 0)
        return (numer_buf, denom_buf, peak_buf)

    initial = (
        jnp.zeros((total_rows, heads_dev * head_dim), jnp.float32),
        jnp.zeros((total_rows, heads_dev), jnp.float32),
        jnp.full((total_rows, heads_dev), MASKED, jnp.float32),
    )
    numer_buf, denom_buf, peak_buf = lax.fori_loop(0, block_total, fill_block, initial)
    width = heads_dev * head_dim + 2 * heads_dev
    packed = jnp.concatenate([numer_buf, denom_buf, peak_buf], axis=1).reshape(
        blk_total, row_count * width
    )
    received = lax.all_to_all(packed, "blk", split_axis=0, concat_axis=0, tiled=True)
    received = received.reshape(blk_total, row_count, width)
    recv_numer = received[:, :, : heads_dev * head_dim]
    recv_denom = received[:, :, heads_dev * head_dim : heads_dev * head_dim + heads_dev]
    recv_peak = received[:, :, heads_dev * head_dim + heads_dev :]
    best = jnp.max(recv_peak, axis=0)
    factor = jnp.exp(recv_peak - best[None])
    summed_denom = jnp.sum(factor * recv_denom, axis=0)
    summed_numer = jnp.sum(
        recv_numer.reshape(blk_total, row_count, heads_dev, head_dim) * factor[:, :, :, None],
        axis=0,
    )
    attended = (summed_numer / summed_denom[:, :, None]).astype(jnp.bfloat16)
    mixed = jnp.einsum("rhd,hde->re", attended, out_fetched, preferred_element_type=jnp.float32)
    head_total = lax.axis_size("head")
    columns = mixed.shape[1] // head_total
    pieces = mixed.astype(jnp.bfloat16).reshape(row_count, head_total, columns)
    pieces = jnp.transpose(pieces, (1, 0, 2))
    exchanged = lax.all_to_all(pieces, "head", split_axis=0, concat_axis=0, tiled=True)
    summed = jnp.sum(exchanged.astype(jnp.float32), axis=0)
    bias_part = lax.dynamic_slice_in_dim(out_bias, lax.axis_index("head") * columns, columns, 0)
    return (summed + bias_part).astype(jnp.bfloat16)


def solution(mesh):
    return jax.shard_map(
        body,
        mesh=mesh,
        in_specs=(
            P("blk", None),
            P("blk", None),
            P(None, "blk", "head", None),
            P(),
            P(),
            P("blk", "head", None),
            P("head", None),
            P("head", "blk", None),
            P(),
            P(),
            P(),
            P(),
            P("blk"),
        ),
        out_specs=P("blk", "head"),
        check_vma=False,
    )
```

profile of v0, /device:TPU:8, one launch (start us, length us, event | category | flops | bytes accessed | tf_op | source)
XLA Modules:
  0.0 287.5 jit_solution(16090769834102768445)
XLA Ops:
  6.5 0.8 copy.52
  7.4 0.9 copy.51
  8.3 0.8 maximum_bitcast_fusion
  9.1 0.8 reduce-window.17
  9.9 0.8 reduce-window.18
  10.7 0.7 reduce.13
  11.6 1.4 fusion.49
  13.0 1.3 fusion.50
  14.3 0.6 concatenate.18
  15.0 0.6 concatenate.19
  15.6 0.7 broadcast_subtract_fusion
  16.3 3.2 %sort.17 = (s32[256]{0:T(256)}, s32[256]{0:T(256)S(1)}) sort(s32[256]{0:T(256)S(1)} %broadcast_subtract_fusion, s32[256]{0:T(256)S(1)} %iota.25), dimensions={0}, to_apply=%region_7.8 | sort | flops 2048 | bytes 4096 | tf_op jit(solution)/shard_map/jit(argsort)/sort | solution.py:51
  19.5 0.6 gather_fusion
  20.1 1.0 convert_reduce_fusion.1
  21.3 1.1 fusion.29
  22.4 0.2 fusion.23
  22.6 91.7 %all-gather.4.cloned.1.call-done = bf16[64,1,32768]{2,1,0:T(2,128)(2,1)} async-done(((bf16[1,1,32768]{2,1,0:T(2,128)(2,1)}), bf16[64,1,32768]{2,1,0:T(2,128)(2,1)}) %all-gather.4.cloned.1.call-update) | async-done | bytes 4194320 | tf_op jit(solution)/shard_map/all_gather | solution.py:57
  114.3 7.9 %copy.55 = bf16[64,1,32768]{2,0,1:T(8,128)(2,1)S(1)} copy(bf16[64,1,32768]{2,1,0:T(2,128)(2,1)} %all-gather.4.cloned.1.call-done) | data formatting | bytes 8388608
  122.2 1.9 copy-done.1
  124.2 1.9 slice.62
  126.0 4.8 %reshape_reshape.3 = bf16[2048,768]{1,0:T(8,128)(2,1)} reshape(bf16[64,24576]{1,0:T(8,128)(2,1)} %slice.62) | data formatting | bytes 6291456 | tf_op jit(solution)/shard_map/reshape;reshape | solution.py:65
  130.9 4.9 %reshape.221 = bf16[2048,1,768]{2,0,1:T(8,128)(2,1)} reshape(bf16[64,24576]{1,0:T(8,128)(2,1)} %slice.62) | data formatting | bytes 6291456 | tf_op jit(solution)/shard_map/reshape | solution.py:59
  135.8 2.6 fusion.19
  138.5 49.4 %all-gather = bf16[1536,1,256]{2,0,1:T(8,128)(2,1)S(1)} all-gather(bf16[24,1,256]{2,0,1:T(8,128)(2,1)S(1)} %get-tuple-element.212), channel_id=2, replica_groups=mesh['head'=8,'blk'=64] {'blk'}, dimensions={0}, use_global_device_ids=true | all-gather | bytes 798720 | tf_op jit(solution)/shard_map/all_gather | solution.py:81
  187.8 0.5 fusion.20
  188.4 0.8 scatter_custom_fusion
  189.2 1.0 scatter_custom_fusion.1
  190.2 0.7 pad_maximum_fusion.1
  190.9 0.6 broadcast_in_dim.64
  191.5 0.6 broadcast_in_dim.65
  192.1 11.9 %while.17 = (s32[]{:T(128)}, f32[1536,256]{1,0:T(8,128)S(1)}, f32[1536,1]{0,1:T(1,128)}, f32[1536,1]{0,1:T(1,128)}, s32[1536]{0:T(1024)}, /*index=5*/s32[280]{0:...) while((s32[]{:T(128)}, f32[1536,256]{1,0:T(8,128)S(1)}, ...), condition=%wide.region_15.16_spmd, body=%wide.region_12.15_spmd.sunk | while | flops 149380608 | bytes 2841579 | solution.py:134
  192.1 0.8 dynamic_slice.29
  192.9 1.0 select_reduce_fusion.2
  193.9 1.4 convolution_dynamic-update-slice_fusion.2
  195.3 0.2 fusion.60
  195.5 0.6 constant_dynamic-update-slice_fusion.3
  196.1 0.8 dynamic_slice.29
  196.8 1.0 select_reduce_fusion.2
  197.8 1.4 convolution_dynamic-update-slice_fusion.2
  199.4 0.6 constant_dynamic-update-slice_fusion.3
  200.0 0.8 dynamic_slice.29
  200.8 1.0 select_reduce_fusion.2
  201.8 1.4 convolution_dynamic-update-slice_fusion.2
  203.4 0.6 constant_dynamic-update-slice_fusion.3
  204.0 1.9 copy.40
  205.9 1.9 copy.39
  207.8 2.2 pad_maximum_fusion
  210.0 4.3 %all_to_all.12 = f32[64,1,6192]{2,1,0:T(1,128)} reshape(f32[1536,258]{1,0:T(8,128)S(1)} %pad_maximum_fusion) | data formatting | bytes 3170304 | tf_op jit(solution)/shard_map/all_to_all | solution.py:139
  214.3 10.0 %all-to-all-start = ((f32[64,1,6192]{2,1,0:T(1,128)}), f32[64,1,6192]{2,1,0:T(1,128)S(1)}, u32[]{:S(2)}, u32[]{:S(2)}) async-start(f32[64,1,6192]{2,1,0:T(1,128)} %all_to_all.12), calls=%async_computation | async-start | bytes 3211264 | tf_op jit(solution)/shard_map/all_to_all | solution.py:139
  224.3 2.3 slice.72
  226.6 2.7 reshape.225
  229.3 25.7 %all-to-all-done = f32[64,1,6192]{2,1,0:T(1,128)S(1)} async-done(((f32[64,1,6192]{2,1,0:T(1,128)}), f32[64,1,6192]{2,1,0:T(1,128)S(1)}, u32[]{:S(2)}, u32[]{:S(2)}) %all-to-all-start) | async-done | bytes 1585184 | tf_op jit(solution)/shard_map/all_to_all | solution.py:139
  255.0 5.4 %reduce.14 = f32[64,6192]{1,0:T(8,128)} reduce(f32[64,1,6192]{2,1,0:T(1,128)S(1)} %all-to-all-done, f32[]{:T(128)} %constant.108), dimensions={1}, to_apply=%all_to_all.10.reduce_sub_computation | reduce | bytes 3170308 | tf_op jit(solution)/shard_map/all_to_all | solution.py:139
  260.4 2.5 reshape.224
  262.9 1.5 fusion.51
  264.4 1.4 copy.48
  265.8 1.4 copy.47
  267.6 0.3 fusion.15
  267.8 1.5 convolution_convert_fusion
  269.3 0.7 copy.56
  270.0 4.3 %all-to-all-start.1 = ((bf16[8,24,256]{2,1,0:T(8,128)(2,1)}), bf16[8,24,256]{2,1,0:T(8,128)(2,1)S(1)}, u32[]{:S(2)}, u32[]{:S(2)}) async-start(bf16[8,24,256]{2,1,0:T(8,128)(2,1)} %bitcast.70), calls=%async_computation.1 | async-start | bytes 196608 | tf_op jit(solution)/shard_map/all_to_all | solution.py:157
  274.2 0.8 dynamic_slice.21
  275.0 5.0 %all-to-all-done.1 = bf16[8,24,256]{2,1,0:T(8,128)(2,1)S(1)} async-done(((bf16[8,24,256]{2,1,0:T(8,128)(2,1)}), bf16[8,24,256]{2,1,0:T(8,128)(2,1)S(1)}, u32[]{:S(2)}, u32[]{:S(2)}) %all-to-all-start.1) | async-done | bytes 98336 | tf_op jit(solution)/shard_map/all_to_all | solution.py:157
  280.1 0.6 add_convert_fusion
  (49 shorter events, 1.2 us)
Async XLA Ops:
  6.5 12.9 %copy-start = (bf16[256,2048]{1,0:T(8,128)(2,1)S(1)}, bf16[256,2048]{1,0:T(8,128)(2,1)}, u32[]{:S(2)}) copy-start(bf16[256,2048]{1,0:T(8,128)(2,1)} %param.16) | copy-start | bytes 3145732
  6.5 16.1 %copy-start.5 = (bf16[2,256,1,256]{3,1,2,0:T(8,128)(2,1)S(1)}, bf16[2,256,1,256]{3,1,2,0:T(8,128)(2,1)}, u32[]{:S(2)}) copy-start(bf16[2,256,1,256]{3,1,2,0:T(8,128)(2,1)} %param.17) | copy-start | bytes 786436
  6.5 107.8 %all-gather.4.cloned.1.call-start = ((), (), s32[]{:S(2)}) async-start(), calls=%async_computation.2 | async-start | bytes 8519680 | tf_op jit(solution)/shard_map/all_gather | solution.py:57
  11.5 1.5 copy-start.7
  122.2 1.9 copy-start.1
  130.9 4.9 %copy-start.4 = (bf16[24,2048]{1,0:T(8,128)(2,1)S(1)}, bf16[24,2048]{1,0:T(8,128)(2,1)}, u32[]{:S(2)}) copy-start(bf16[24,2048]{1,0:T(8,128)(2,1)} %param.15) | copy-start | bytes 294916
  130.9 4.9 %copy-start.8 = (f32[2048]{0:T(1024)S(1)}, f32[2048]{0:T(1024)}, u32[]{:S(2)}) copy-start(f32[2048]{0:T(1024)} %param.19) | copy-start | bytes 24580
  130.9 4.9 %copy-start.9 = (f32[2048]{0:T(1024)S(1)}, f32[2048]{0:T(1024)}, u32[]{:S(2)}) copy-start(f32[2048]{0:T(1024)} %param.18) | copy-start | bytes 24580
  135.8 52.0 %copy-start.3 = (bf16[2048,1,768]{2,0,1:T(8,128)(2,1)S(1)}, bf16[2048,1,768]{2,0,1:T(8,128)(2,1)}, u32[]{:S(2)}) copy-start(bf16[2048,1,768]{2,0,1:T(8,128)(2,1)} %reshape.221) | copy-start | bytes 9437188
  135.8 52.0 %slice-start = ((f32[1,768]{1,0:T(1,128)}), f32[1,512]{1,0:T(1,128)S(1)}, s32[]{:S(2)}) async-start(f32[1,768]{1,0:T(1,128)} %param.21), calls=%async_computation.3 | async-start | bytes 4096 | tf_op jit(solution)/shard_map/slice | solution.py:76
  192.1 3.1 %copy-start.6 = (s32[280]{0:T(512)S(1)}, s32[280]{0:T(512)}, u32[]{:S(2)}) copy-start(s32[280]{0:T(512)} %get-tuple-element.320) | copy-start | bytes 3364 | tf_op jit(solution)/shard_map/while
  196.1 3.1 %copy-start.6 = (s32[280]{0:T(512)S(1)}, s32[280]{0:T(512)}, u32[]{:S(2)}) copy-start(s32[280]{0:T(512)} %get-tuple-element.320) | copy-start | bytes 3364 | tf_op jit(solution)/shard_map/while
  200.0 3.2 %copy-start.6 = (s32[280]{0:T(512)S(1)}, s32[280]{0:T(512)}, u32[]{:S(2)}) copy-start(s32[280]{0:T(512)} %get-tuple-element.320) | copy-start | bytes 3364 | tf_op jit(solution)/shard_map/while
  204.0 3.8 %copy-start.2 = (f32[1536,256]{1,0:T(8,128)}, f32[1536,256]{1,0:T(8,128)S(1)}, u32[]{:S(2)}) copy-start(f32[1536,256]{1,0:T(8,128)S(1)} %get-tuple-element.178) | copy-start | bytes 4718596
  214.3 40.7 %all-to-all-start = ((f32[64,1,6192]{2,1,0:T(1,128)}), f32[64,1,6192]{2,1,0:T(1,128)S(1)}, u32[]{:S(2)}, u32[]{:S(2)}) async-start(f32[64,1,6192]{2,1,0:T(1,128)} %all_to_all.12), calls=%async_computation | async-start | bytes 3211264 | tf_op jit(solution)/shard_map/all_to_all | solution.py:139
  270.0 10.1 %all-to-all-start.1 = ((bf16[8,24,256]{2,1,0:T(8,128)(2,1)}), bf16[8,24,256]{2,1,0:T(8,128)(2,1)S(1)}, u32[]{:S(2)}, u32[]{:S(2)}) async-start(bf16[8,24,256]{2,1,0:T(8,128)(2,1)} %bitcast.70), calls=%async_computation.1 | async-start | bytes 196608 | tf_op jit(solution)/shard_map/all_to_all | solution.py:157
Sparse Core Ops, SparseCore 0:
  10.4 103.9 all-gather.3
where the time goes:
time: 289 us; the launch traced here: 288 us
  waiting for transfers between devices  122 us (42%)
  local copies, waits for them, and re-layouts  52.2 us (18%)
  blocking collectives  49.4 us (17%)
  other arithmetic  23.7 us (8%)
  starting transfers between devices  14.3 us (5%)
  between operations  13.6 us (5%)
  matrix products  11.7 us (4%)
    all_gather x1, waiting for transfers between devices, body(): fetched_all = lax.all_gather(packed_weights, 'blk', axis=0, tiled=True)  91.7 us
    all_gather x1, blocking collectives, body(): gathered = lax.all_gather(own_queries, 'blk', axis=0, tiled=True)  49.4 us
    all_to_all x1, waiting for transfers between devices, body(): lax.all_to_all(packed, 'blk', split_axis=0, concat_axis=0, tiled=True)  25.7 us
    unnamed x23, local copies, waits for them, and re-layouts  14.4 us
    all_to_all x1, starting transfers between devices, body(): lax.all_to_all(packed, 'blk', split_axis=0, concat_axis=0, tiled=True)  10 us
  transfers between devices with their start and end apart: 3, of which 3 were waited for; matrix products, arithmetic and copies ran while one was open for 7% of the time, Pallas kernels for 0%

commit v1 on v0

--- a/solution.py
+++ b/solution.py
@@ -7,6 +7,10 @@
 FLAG_DEV = 25
 EPSILON = 1e-05
 MASKED = -1e30
+positions_extend = lambda field, array_axis: jnp.concatenate(
+    jax.lax.all_to_all(jnp.stack(jax.lax.axis_size("blk") * [field], axis=0), "blk", 0, 0),
+    array_axis,
+)
 
 
 def layer_norm(states, norm_scale, norm_shift):
@@ -78,7 +82,7 @@
         .reshape(FLAG_DEV, heads_dev, 2 * head_dim)
     )
     own_queries = projected[:, :, :head_dim].reshape(row_count, heads_dev * head_dim)
-    gathered = lax.all_gather(own_queries, "blk", axis=0, tiled=True)
+    gathered = positions_extend(own_queries, 0)
     prefix_keys = kv_cache[0].at[flagged].set(recomputed[:, :, :head_dim])
     prefix_values = kv_cache[1].at[flagged].set(recomputed[:, :, head_dim:])
     keys_all = jnp.concatenate([prefix_keys, projected[:, :, head_dim : 2 * head_dim]], axis=0)

time: 289 us -> 274 us (0.948)
  the two profiles are of different devices: /device:TPU:8 before, /device:TPU:1 now
where the time goes in v1:
time: 274 us; the launch traced here: 273 us
  waiting for transfers between devices  142 us (52%)
  local copies, waits for them, and re-layouts  53.1 us (19%)
  starting transfers between devices  27.6 us (10%)
  other arithmetic  23.7 us (9%)
  between operations  13.6 us (5%)
  matrix products  13.2 us (5%)
    all_gather x1, waiting for transfers between devices, body(): fetched_all = lax.all_gather(packed_weights, 'blk', axis=0, tiled=True)  93.7 us
    all_to_all x1, waiting for transfers between devices, body(): lax.all_to_all(packed, 'blk', split_axis=0, concat_axis=0, tiled=True)  32.9 us
    unnamed x21, local copies, waits for them, and re-layouts  14.4 us
    all_to_all x1, waiting for transfers between devices, jax.lax.all_to_all(jnp.stack(jax.lax.axis_size('blk') * [field], axis=0),...  10.7 us
    all_to_all x1, starting transfers between devices, jax.lax.all_to_all(jnp.stack(jax.lax.axis_size('blk') * [field], axis=0),...  9.79 us
    all_to_all x1, starting transfers between devices, body(): lax.all_to_all(packed, 'blk', split_axis=0, concat_axis=0, tiled=True)  9.26 us
    all_to_all x1, starting transfers between devices, body(): lax.all_to_all(pieces, 'head', split_axis=0, concat_axis=0, tiled=True)  8.58 us
  transfers between devices with their start and end apart: 4, of which 4 were waited for; matrix products, arithmetic and copies ran while one was open for 10% of the time, Pallas kernels for 0%

profile of v1, /device:TPU:1, one launch (start us, length us, event | category | flops | bytes accessed | tf_op | source)
XLA Modules:
  0.0 272.9 jit_solution(16990334677357716392)
XLA Ops:
  6.5 0.8 copy.52
  7.4 0.9 copy.51
  8.3 0.8 maximum_bitcast_fusion
  9.1 0.8 reduce-window.17
  9.9 0.8 reduce-window.18
  10.7 0.7 reduce.13
  11.6 1.4 fusion.49
  13.0 1.3 fusion.50
  14.3 0.6 concatenate.18
  15.0 0.6 concatenate.19
  15.6 0.7 broadcast_subtract_fusion
  16.2 3.2 %sort.17 = (s32[256]{0:T(256)}, s32[256]{0:T(256)S(1)}) sort(s32[256]{0:T(256)S(1)} %broadcast_subtract_fusion, s32[256]{0:T(256)S(1)} %iota.25), dimensions={0}, to_apply=%region_7.8 | sort | flops 2048 | bytes 4096 | tf_op jit(solution)/shard_map/jit(argsort)/sort | solution.py:55
  19.4 1.0 convert_reduce_fusion.1
  20.5 1.1 fusion.29
  21.6 93.7 %all-gather.3.cloned.1.call-done = bf16[64,1,32768]{2,1,0:T(2,128)(2,1)} async-done(((bf16[1,1,32768]{2,1,0:T(2,128)(2,1)}), bf16[64,1,32768]{2,1,0:T(2,128)(2,1)}) %all-gather.3.cloned.1.call-update) | async-done | bytes 4194320 | tf_op jit(solution)/shard_map/all_gather | solution.py:61
  115.2 7.9 %copy.55 = bf16[64,1,32768]{2,0,1:T(8,128)(2,1)S(1)} copy(bf16[64,1,32768]{2,1,0:T(2,128)(2,1)} %all-gather.3.cloned.1.call-done) | data formatting | bytes 8388608
  123.2 1.9 copy-done.1
  125.1 1.9 slice.62
  127.0 4.9 %reshape_reshape.3 = bf16[2048,768]{1,0:T(8,128)(2,1)} reshape(bf16[64,24576]{1,0:T(8,128)(2,1)} %slice.62) | data formatting | bytes 6291456 | tf_op jit(solution)/shard_map/reshape;reshape | solution.py:69
  131.8 2.5 fusion.19
  134.3 0.9 stack.3
  135.3 9.8 %all-to-all-start = ((bf16[64,24,256]{2,1,0:T(8,128)(2,1)}), bf16[64,24,256]{2,1,0:T(8,128)(2,1)S(1)}, u32[]{:S(2)}, u32[]{:S(2)}) async-start(bf16[64,24,256]{2,1,0:T(8,128)(2,1)} %stack.3), calls=%async_computation | async-start | bytes 1572864 | tf_op jit(solution)/shard_map/all_to_all | solution.py:11
  145.1 0.6 gather_fusion
  146.1 4.8 %reshape.223 = bf16[2048,1,768]{2,0,1:T(8,128)(2,1)} reshape(bf16[64,24576]{1,0:T(8,128)(2,1)} %slice.62) | data formatting | bytes 6291456 | tf_op jit(solution)/shard_map/reshape | solution.py:63
  151.0 2.1 fusion.20
  153.1 0.8 scatter_custom_fusion
  153.9 1.0 scatter_custom_fusion.1
  154.9 0.7 pad_maximum_fusion.1
  155.6 10.7 %all-to-all-done = bf16[64,24,256]{2,1,0:T(8,128)(2,1)S(1)} async-done(((bf16[64,24,256]{2,1,0:T(8,128)(2,1)}), bf16[64,24,256]{2,1,0:T(8,128)(2,1)S(1)}, u32[]{:S(2)}, u32[]{:S(2)}) %all-to-all-start) | async-done | bytes 786464 | tf_op jit(solution)/shard_map/all_to_all | solution.py:11
  166.3 0.6 broadcast_in_dim.64
  166.9 0.6 broadcast_in_dim.65
  167.5 11.9 %while.17 = (s32[]{:T(128)}, f32[1536,256]{1,0:T(8,128)S(1)}, f32[1536,1]{0,1:T(1,128)}, f32[1536,1]{0,1:T(1,128)}, s32[1536]{0:T(1024)}, /*index=5*/s32[280]{0:...) while((s32[]{:T(128)}, f32[1536,256]{1,0:T(8,128)S(1)}, ...), condition=%wide.region_15.16_spmd, body=%wide.region_12.15_spmd.sunk | while | flops 149380608 | bytes 2841579 | solution.py:138
  167.6 0.8 dynamic_slice.29
  168.3 1.0 select_reduce_fusion.2
  169.3 1.4 convolution_dynamic-update-slice_fusion.2
  170.9 0.6 constant_dynamic-update-slice_fusion.3
  171.5 0.8 dynamic_slice.29
  172.3 1.0 select_reduce_fusion.2
  173.3 1.4 convolution_dynamic-update-slice_fusion.2
  174.8 0.6 constant_dynamic-update-slice_fusion.3
  175.5 0.8 dynamic_slice.29
  176.2 1.0 select_reduce_fusion.2
  177.2 1.4 convolution_dynamic-update-slice_fusion.2
  178.8 0.6 constant_dynamic-update-slice_fusion.3
  179.4 1.9 copy.40
  181.3 1.9 copy.39
  183.2 2.2 pad_maximum_fusion
  185.4 4.3 %all_to_all.16 = f32[64,1,6192]{2,1,0:T(1,128)} reshape(f32[1536,258]{1,0:T(8,128)S(1)} %pad_maximum_fusion) | data formatting | bytes 3170304 | tf_op jit(solution)/shard_map/all_to_all | solution.py:143
  189.7 9.3 %all-to-all-start.1 = ((f32[64,1,6192]{2,1,0:T(1,128)}), f32[64,1,6192]{2,1,0:T(1,128)S(1)}, u32[]{:S(2)}, u32[]{:S(2)}) async-start(f32[64,1,6192]{2,1,0:T(1,128)} %all_to_all.16), calls=%async_computation.1 | async-start | bytes 3211264 | tf_op jit(solution)/shard_map/all_to_all | solution.py:143
  199.0 2.3 slice.72
  201.2 2.7 reshape.227
  203.9 32.9 %all-to-all-done.1 = f32[64,1,6192]{2,1,0:T(1,128)S(1)} async-done(((f32[64,1,6192]{2,1,0:T(1,128)}), f32[64,1,6192]{2,1,0:T(1,128)S(1)}, u32[]{:S(2)}, u32[]{:S(2)}) %all-to-all-start.1) | async-done | bytes 1585184 | tf_op jit(solution)/shard_map/all_to_all | solution.py:143
  236.9 5.4 %reduce.14 = f32[64,6192]{1,0:T(8,128)} reduce(f32[64,1,6192]{2,1,0:T(1,128)S(1)} %all-to-all-done.1, f32[]{:T(128)} %constant.108), dimensions={1}, to_apply=%all_to_all.14.reduce_sub_computation | reduce | bytes 3170308 | tf_op jit(solution)/shard_map/all_to_all | solution.py:143
  242.2 2.5 reshape.226
  244.8 1.5 fusion.51
  246.3 1.4 copy.48
  247.7 1.4 copy.47
  249.4 0.3 fusion.15
  249.7 1.5 convolution_convert_fusion
  251.2 0.7 copy.56
  251.9 8.6 %all-to-all-start.2 = ((bf16[8,24,256]{2,1,0:T(8,128)(2,1)}), bf16[8,24,256]{2,1,0:T(8,128)(2,1)S(1)}, u32[]{:S(2)}, u32[]{:S(2)}) async-start(bf16[8,24,256]{2,1,0:T(8,128)(2,1)} %bitcast.72), calls=%async_computation.2 | async-start | bytes 196608 | tf_op jit(solution)/shard_map/all_to_all | solution.py:161
  260.5 0.8 dynamic_slice.21
  261.2 4.2 %all-to-all-done.2 = bf16[8,24,256]{2,1,0:T(8,128)(2,1)S(1)} async-done(((bf16[8,24,256]{2,1,0:T(8,128)(2,1)}), bf16[8,24,256]{2,1,0:T(8,128)(2,1)S(1)}, u32[]{:S(2)}, u32[]{:S(2)}) %all-to-all-start.2) | async-done | bytes 98336 | tf_op jit(solution)/shard_map/all_to_all | solution.py:161
  265.5 0.6 add_convert_fusion
  (49 shorter events, 1.6 us)
Async XLA Ops:
  6.5 138.6 %copy-start = (bf16[256,2048]{1,0:T(8,128)(2,1)S(1)}, bf16[256,2048]{1,0:T(8,128)(2,1)}, u32[]{:S(2)}) copy-start(bf16[256,2048]{1,0:T(8,128)(2,1)} %param.16) | copy-start | bytes 3145732
  6.5 108.7 %all-gather.3.cloned.1.call-start = ((), (), s32[]{:S(2)}) async-start(), calls=%async_computation.3 | async-start | bytes 8519680 | tf_op jit(solution)/shard_map/all_gather | solution.py:61
  11.5 1.5 copy-start.6
  123.1 1.9 copy-start.1
  127.0 4.9 %copy-start.3 = (bf16[24,2048]{1,0:T(8,128)(2,1)S(1)}, bf16[24,2048]{1,0:T(8,128)(2,1)}, u32[]{:S(2)}) copy-start(bf16[24,2048]{1,0:T(8,128)(2,1)} %param.15) | copy-start | bytes 294916
  127.0 4.9 %copy-start.7 = (f32[2048]{0:T(1024)S(1)}, f32[2048]{0:T(1024)}, u32[]{:S(2)}) copy-start(f32[2048]{0:T(1024)} %param.19) | copy-start | bytes 24580
  127.0 4.9 %copy-start.8 = (f32[2048]{0:T(1024)S(1)}, f32[2048]{0:T(1024)}, u32[]{:S(2)}) copy-start(f32[2048]{0:T(1024)} %param.18) | copy-start | bytes 24580
  134.3 11.8 %copy-start.4 = (bf16[2,256,1,256]{3,1,2,0:T(8,128)(2,1)S(1)}, bf16[2,256,1,256]{3,1,2,0:T(8,128)(2,1)}, u32[]{:S(2)}) copy-start(bf16[2,256,1,256]{3,1,2,0:T(8,128)(2,1)} %param.17) | copy-start | bytes 786436
  135.3 31.0 %all-to-all-start = ((bf16[64,24,256]{2,1,0:T(8,128)(2,1)}), bf16[64,24,256]{2,1,0:T(8,128)(2,1)S(1)}, u32[]{:S(2)}, u32[]{:S(2)}) async-start(bf16[64,24,256]{2,1,0:T(8,128)(2,1)} %stack.3), calls=%async_computation | async-start | bytes 1572864 | tf_op jit(solution)/shard_map/all_to_all | solution.py:11
  146.1 4.8 %slice-start = ((f32[1,768]{1,0:T(1,128)}), f32[1,512]{1,0:T(1,128)S(1)}, s32[]{:S(2)}) async-start(f32[1,768]{1,0:T(1,128)} %param.21), calls=%async_computation.4 | async-start | bytes 4096 | tf_op jit(solution)/shard_map/slice | solution.py:80
  167.5 3.1 %copy-start.5 = (s32[280]{0:T(512)S(1)}, s32[280]{0:T(512)}, u32[]{:S(2)}) copy-start(s32[280]{0:T(512)} %get-tuple-element.320) | copy-start | bytes 3364 | tf_op jit(solution)/shard_map/while
  171.5 3.1 %copy-start.5 = (s32[280]{0:T(512)S(1)}, s32[280]{0:T(512)}, u32[]{:S(2)}) copy-start(s32[280]{0:T(512)} %get-tuple-element.320) | copy-start | bytes 3364 | tf_op jit(solution)/shard_map/while
  175.4 3.1 %copy-start.5 = (s32[280]{0:T(512)S(1)}, s32[280]{0:T(512)}, u32[]{:S(2)}) copy-start(s32[280]{0:T(512)} %get-tuple-element.320) | copy-start | bytes 3364 | tf_op jit(solution)/shard_map/while
  179.4 3.8 %copy-start.2 = (f32[1536,256]{1,0:T(8,128)}, f32[1536,256]{1,0:T(8,128)S(1)}, u32[]{:S(2)}) copy-start(f32[1536,256]{1,0:T(8,128)S(1)} %get-tuple-element.178) | copy-start | bytes 4718596
  189.7 47.2 %all-to-all-start.1 = ((f32[64,1,6192]{2,1,0:T(1,128)}), f32[64,1,6192]{2,1,0:T(1,128)S(1)}, u32[]{:S(2)}, u32[]{:S(2)}) async-start(f32[64,1,6192]{2,1,0:T(1,128)} %all_to_all.16), calls=%async_computation.1 | async-start | bytes 3211264 | tf_op jit(solution)/shard_map/all_to_all | solution.py:143
  251.9 13.6 %all-to-all-start.2 = ((bf16[8,24,256]{2,1,0:T(8,128)(2,1)}), bf16[8,24,256]{2,1,0:T(8,128)(2,1)S(1)}, u32[]{:S(2)}, u32[]{:S(2)}) async-start(bf16[8,24,256]{2,1,0:T(8,128)(2,1)} %bitcast.72), calls=%async_computation.2 | async-start | bytes 196608 | tf_op jit(solution)/shard_map/all_to_all | solution.py:161
Sparse Core Ops, SparseCore 0:
  10.4 104.8 all-gather.2
